TPU v7x, 32 devices: a whole 2x2x4 slice. The times are simulated.
32 devices in a mesh: batch: 8 (over z, y), tensor: 4 (over x, core).
Axes of the slice: x: 2, y: 2, z: 4, core: 2. Of those that a mesh axis runs over, the one named last changes fastest.
Arguments:
- tokens: bfloat16 [12288, 768], P('batch'), may hold values from -6 to 6
- lengths: int32 [8], P('batch'), may hold values from 1024 to 1536, as said below
- w_query: bfloat16 [768, 768], P('batch', 'tensor'), may hold values from -0.4375 to 0.4375
- w_key: bfloat16 [768, 768], P('batch', 'tensor'), may hold values from -0.21875 to 0.21875
- w_value: bfloat16 [768, 768], P('batch', 'tensor'), may hold values from -0.21875 to 0.21875
- w_out: bfloat16 [768, 768], P('tensor', 'batch'), may hold values from -0.875 to 0.875
- w_up: bfloat16 [768, 3072], P('batch', 'tensor'), may hold values from -0.21875 to 0.21875
- w_down: bfloat16 [3072, 768], P('tensor', 'batch'), may hold values from -0.109375 to 0.109375
- norm_gain: bfloat16 [2, 768], P(None, 'batch'), may hold values from 0.099609375 to 1.8984375
- norm_shift: bfloat16 [2, 768], P(None, 'batch'), may hold values from -3 to 3
- out_grad: bfloat16 [12288, 768], P('batch'), may hold values from -6 to 6
Outputs:
- layer_out: bfloat16 [12288, 768], P('batch')
- grad_input: bfloat16 [12288, 768], P('batch')
- grad_query: float32 [768, 768], P('batch', 'tensor')
- grad_key: float32 [768, 768], P('batch', 'tensor')
- grad_value: float32 [768, 768], P('batch', 'tensor')
- grad_out: float32 [768, 768], P('tensor', 'batch')
- grad_up: float32 [768, 3072], P('batch', 'tensor')
- grad_down: float32 [3072, 768], P('tensor', 'batch')
- grad_gain: float32 [2, 768], P(None, 'batch')
- grad_shift: float32 [2, 768], P(None, 'batch')
Inputs may be any that keep to these rules, and one draw needn't show every extreme that they name: `lengths`: each sequence's valid tokens; some sequence fills all 1536 slots.
All inputs are finite; a program needn't handle non-finite values.
Results may differ from a plain program's by a relative error of at most 0.017.
Values may be sent and summed in bfloat16 or wider, within the bound.
No kernel may reach another device: no remote copies, remote signals or barrier semaphores. Data moves between devices by JAX's collectives and lax.ppermute only.
A program may use at most 192 MiB of HBM per device.

v0:
```python
import jax
import jax.numpy as jnp
from jax import lax
from jax.sharding import PartitionSpec as P

HD = 64
epsilon = 1e-05


def cut_along(value, dim, length):
    shape = value.shape
    parts = value.reshape(*shape[:dim], length, shape[dim] // length, *shape[dim + 1 :])
    return jnp.moveaxis(parts, dim, 0)


def summed_on_arrival(value, axis, dim):
    length = lax.axis_size(axis)
    parts = lax.all_to_all(cut_along(value, dim, length), axis, 0, 0, tiled=True)
    return jnp.sum(parts.astype(jnp.float32), axis=0)


def normalize_keep(values, gain_row, shift_row):
    middle = jnp.mean(values, axis=-1, keepdims=True)
    centred = values - middle
    spread = jnp.mean(centred * centred, axis=-1, keepdims=True)
    inverse = lax.rsqrt(spread + epsilon)
    scaled = centred * inverse
    return (scaled * gain_row + shift_row, scaled, inverse)


def normalize_back(grad_normed, scaled, inverse, gain_row):
    grad_scaled = grad_normed * gain_row
    mean_grad = jnp.mean(grad_scaled, axis=-1, keepdims=True)
    mean_cross = jnp.mean(grad_scaled * scaled, axis=-1, keepdims=True)
    grad_values = inverse * (grad_scaled - mean_grad - scaled * mean_cross)
    return (grad_values, jnp.sum(grad_normed * scaled, axis=0), jnp.sum(grad_normed, axis=0))


def multiply(left_mat, right_mat):
    return jnp.dot(left_mat, right_mat, preferred_element_type=jnp.float32)


def inner_rows(left_mat, right_mat):
    return lax.dot_general(
        left_mat, right_mat, (((0,), (0,)), ((), ())), preferred_element_type=jnp.float32
    )


def outer_cols(left_mat, right_mat):
    return lax.dot_general(
        left_mat, right_mat, (((1,), (1,)), ((), ())), preferred_element_type=jnp.float32
    )


def gelu_tanh(values):
    return jax.nn.gelu(values, approximate=True)


def score_block(queries_blk, keys_part, row_pos, key_pos, length, scaling):
    raw_scores = jnp.einsum(
        "qhd,khd->hqk", queries_blk, keys_part, preferred_element_type=jnp.float32
    )
    scores = raw_scores * scaling
    allowed = (key_pos[None, :] <= row_pos[:, None]) & (key_pos[None, :] < length)
    magnitude = jnp.where(allowed[None], jnp.abs(scores), -1e30)
    return (scores, magnitude)


def attend_forward(queries, key_rows, value_rows, length, block_rows, scaling):
    seq_rows = queries.shape[0]
    position = jnp.arange(seq_rows, dtype=jnp.int32)
    outputs = []
    log_sums = []
    for number in range(seq_rows // block_rows):
        begin_row = number * block_rows
        end_row = begin_row + block_rows
        scores, magnitude = score_block(
            queries[begin_row:end_row],
            key_rows[:end_row],
            position[begin_row:end_row],
            position[:end_row],
            length,
            scaling,
        )
        row_max = jnp.max(magnitude, axis=-1, keepdims=True)
        exponent = jnp.exp(magnitude - row_max)
        row_sum = jnp.sum(exponent, axis=-1, keepdims=True)
        weights = (jnp.sign(scores) * (exponent / row_sum)).astype(jnp.bfloat16)
        outputs.append(
            jnp.einsum(
                "hqk,khd->qhd", weights, value_rows[:end_row], preferred_element_type=jnp.float32
            )
        )
        log_sums.append(row_max + jnp.log(row_sum))
    return (jnp.concatenate(outputs, axis=0), jnp.concatenate(log_sums, axis=1))


def attend_back(queries, key_rows, value_rows, grad_mixed, log_sums, length, block_rows, scaling):
    seq_rows = queries.shape[0]
    position = jnp.arange(seq_rows, dtype=jnp.int32)
    grad_queries = []
    grad_keys = jnp.zeros(key_rows.shape, jnp.float32)
    grad_values = jnp.zeros(value_rows.shape, jnp.float32)
    for number in range(seq_rows // block_rows):
        begin_row = number * block_rows
        end_row = begin_row + block_rows
        scores, magnitude = score_block(
            queries[begin_row:end_row],
            key_rows[:end_row],
            position[begin_row:end_row],
            position[:end_row],
            length,
            scaling,
        )
        probability = jnp.exp(magnitude - log_sums[:, begin_row:end_row])
        signs = jnp.sign(scores)
        weights = signs * probability
        grad_blk = grad_mixed[begin_row:end_row]
        grad_weights = jnp.einsum(
            "qhd,khd->hqk", grad_blk, value_rows[:end_row], preferred_element_type=jnp.float32
        )
        delta_row = jnp.sum(weights * grad_weights, axis=-1, keepdims=True)
        grad_raw = (signs * probability * (signs * grad_weights - delta_row) * scaling).astype(
            jnp.bfloat16
        )
        grad_queries.append(
            jnp.einsum(
                "hqk,khd->qhd", grad_raw, key_rows[:end_row], preferred_element_type=jnp.float32
            )
        )
        grad_keys = grad_keys.at[:end_row].add(
            jnp.einsum(
                "hqk,qhd->khd",
                grad_raw,
                queries[begin_row:end_row],
                preferred_element_type=jnp.float32,
            )
        )
        grad_values = grad_values.at[:end_row].add(
            jnp.einsum(
                "hqk,qhd->khd",
                weights.astype(jnp.bfloat16),
                grad_blk,
                preferred_element_type=jnp.float32,
            )
        )
    return (jnp.concatenate(grad_queries, axis=0), grad_keys, grad_values)


def per_device(
    tokens, lengths, w_query, w_key, w_value, w_out, w_up, w_down, norm_gain, norm_shift, out_grad
):
    seq_rows = tokens.shape[0]
    seq_count = lengths.shape[0]
    seq_len = seq_rows // seq_count
    position = jnp.arange(seq_rows, dtype=jnp.int32)
    slot_length = jnp.repeat(lengths, seq_len)
    is_valid = (position % seq_len < slot_length).astype(jnp.float32)[:, None]
    block_rows = min(512, seq_len)
    scaling = float(HD) ** (-0.5)
    gathered = (
        lax.all_gather(w_query, "batch", axis=0, tiled=True),
        lax.all_gather(w_key, "batch", axis=0, tiled=True),
        lax.all_gather(w_value, "batch", axis=0, tiled=True),
        lax.all_gather(w_out, "batch", axis=1, tiled=True),
        lax.all_gather(w_up, "batch", axis=0, tiled=True),
        lax.all_gather(w_down, "batch", axis=1, tiled=True),
        lax.all_gather(norm_gain, "batch", axis=1, tiled=True),
        lax.all_gather(norm_shift, "batch", axis=1, tiled=True),
    )
    full_query, full_key, full_value, full_out, full_up, full_down, gain_full, shift_full = gathered
    gain_rows = gain_full.astype(jnp.float32)
    shift_rows = shift_full.astype(jnp.float32)
    head_count = full_query.shape[1] // HD

    def per_sequence(values):
        return values.reshape(seq_count, seq_len, head_count, HD)

    inputs = tokens.astype(jnp.float32)
    normed, scaled_one, inverse_one = normalize_keep(inputs, gain_rows[0], shift_rows[0])
    normed_low = normed.astype(jnp.bfloat16)
    queries = (
        multiply(normed_low, full_query).astype(jnp.bfloat16).reshape(seq_rows, head_count, HD)
    )
    key_rows = multiply(normed_low, full_key).astype(jnp.bfloat16).reshape(seq_rows, head_count, HD)
    value_rows = (
        multiply(normed_low, full_value).astype(jnp.bfloat16).reshape(seq_rows, head_count, HD)
    )

    def forward_one(items):
        return attend_forward(items[0], items[1], items[2], items[3], block_rows, scaling)

    mixed_heads, log_sums = lax.map(
        forward_one,
        (per_sequence(queries), per_sequence(key_rows), per_sequence(value_rows), lengths),
    )
    mixed_low = mixed_heads.reshape(seq_rows, head_count * HD).astype(jnp.bfloat16)
    attn_partial = multiply(mixed_low, full_out)
    hidden = inputs + lax.psum(attn_partial, "tensor")
    normed_two, scaled_two, inverse_two = normalize_keep(hidden, gain_rows[1], shift_rows[1])
    normed_two_low = normed_two.astype(jnp.bfloat16)
    up_proj = multiply(normed_two_low, full_up)
    active_full, gelu_pull = jax.vjp(gelu_tanh, up_proj)
    active = active_full.astype(jnp.bfloat16)
    down_partial = multiply(active, full_down)
    branch = lax.psum(down_partial.astype(jnp.bfloat16), "tensor").astype(jnp.float32)
    out_rows = ((hidden + branch) * is_valid).astype(jnp.bfloat16)
    grad_rows = out_grad * is_valid.astype(jnp.bfloat16)
    grad_down = inner_rows(active, grad_rows)
    grad_active = outer_cols(grad_rows, full_down)
    grad_upper = gelu_pull(grad_active)[0].astype(jnp.bfloat16)
    grad_up = inner_rows(normed_two_low, grad_upper)
    mid_partial = outer_cols(grad_upper, full_up)
    grad_normed_two = lax.psum(mid_partial, "tensor")
    grad_from_two, gain_two, shift_two = normalize_back(
        grad_normed_two, scaled_two, inverse_two, gain_rows[1]
    )
    grad_hidden = grad_rows.astype(jnp.float32) + grad_from_two
    grad_attn = grad_hidden.astype(jnp.bfloat16)
    grad_out = inner_rows(mixed_low, grad_attn)
    grad_mixed = (
        outer_cols(grad_attn, full_out).astype(jnp.bfloat16).reshape(seq_rows, head_count, HD)
    )

    def backward_one(items):
        return attend_back(
            items[0], items[1], items[2], items[3], items[4], items[5], block_rows, scaling
        )

    grad_queries, grad_keys, grad_values = lax.map(
        backward_one,
        (
            per_sequence(queries),
            per_sequence(key_rows),
            per_sequence(value_rows),
            per_sequence(grad_mixed),
            log_sums,
            lengths,
        ),
    )
    queries_low = grad_queries.astype(jnp.bfloat16).reshape(seq_rows, head_count * HD)
    keys_low = grad_keys.astype(jnp.bfloat16).reshape(seq_rows, head_count * HD)
    values_low = grad_values.astype(jnp.bfloat16).reshape(seq_rows, head_count * HD)
    grad_query = inner_rows(normed_low, queries_low)
    grad_key = inner_rows(normed_low, keys_low)
    grad_value = inner_rows(normed_low, values_low)
    partial_in = (
        outer_cols(queries_low, full_query)
        + outer_cols(keys_low, full_key)
        + outer_cols(values_low, full_value)
    )
    grad_normed = lax.psum(partial_in.astype(jnp.bfloat16), "tensor").astype(jnp.float32)
    grad_from_one, gain_one, shift_one = normalize_back(
        grad_normed, scaled_one, inverse_one, gain_rows[0]
    )
    grad_input = (grad_hidden + grad_from_one).astype(jnp.bfloat16)
    gain_pair = jnp.stack([gain_one, gain_two])
    shift_pair = jnp.stack([shift_one, shift_two])
    everything = (
        summed_on_arrival(grad_query.astype(jnp.bfloat16), "batch", 0),
        summed_on_arrival(grad_key.astype(jnp.bfloat16), "batch", 0),
        summed_on_arrival(grad_value.astype(jnp.bfloat16), "batch", 0),
        summed_on_arrival(grad_out.astype(jnp.bfloat16), "batch", 1),
        summed_on_arrival(grad_up.astype(jnp.bfloat16), "batch", 0),
        summed_on_arrival(grad_down.astype(jnp.bfloat16), "batch", 1),
        summed_on_arrival(gain_pair.astype(jnp.bfloat16), "batch", 1),
        summed_on_arrival(shift_pair.astype(jnp.bfloat16), "batch", 1),
    )
    (
        shard_query,
        shard_key,
        shard_value,
        shard_out,
        shard_up,
        shard_down,
        shard_gain,
        shard_shift,
    ) = everything
    return (
        out_rows,
        grad_input,
        shard_query,
        shard_key,
        shard_value,
        shard_out,
        shard_up,
        shard_down,
        shard_gain,
        shard_shift,
    )


def solution(mesh):
    in_specs = (
        P("batch", None),
        P("batch"),
        P("batch", "tensor"),
        P("batch", "tensor"),
        P("batch", "tensor"),
        P("tensor", "batch"),
        P("batch", "tensor"),
        P("tensor", "batch"),
        P(None, "batch"),
        P(None, "batch"),
        P("batch", None),
    )
    out_specs = (
        P("batch", None),
        P("batch", None),
        P("batch", "tensor"),
        P("batch", "tensor"),
        P("batch", "tensor"),
        P("tensor", "batch"),
        P("batch", "tensor"),
        P("tensor", "batch"),
        P(None, "batch"),
        P(None, "batch"),
    )
    return jax.shard_map(
        per_device, mesh=mesh, in_specs=in_specs, out_specs=out_specs, check_vma=False
    )
```

profile of v0, /device:TPU:0, one launch (start us, length us, event | category | flops | bytes accessed | tf_op | source)
XLA Modules:
  0.0 746.9 jit_solution(5650384383720290563)
XLA Ops:
  9.3 22.3 %all-gather = bf16[8,96,2]{1,2,0:T(2,128)(2,1)S(1)} all-gather(bf16[1,96,2]{1,2,0:T(2,128)(2,1)} %bitcast.189), channel_id=1, replica_groups=mesh['batch'=8,'tensor'=4] {'batch'}, dimensions={0}, use_global_device_ids=true | all-gather | bytes 3456 | tf_op jit(solution)/shard_map/all_gather | solution.py:168
  32.3 16.4 %all-gather.1 = bf16[8,96,2]{1,2,0:T(2,128)(2,1)S(1)} all-gather(bf16[1,96,2]{1,2,0:T(2,128)(2,1)} %bitcast.190), channel_id=1, replica_groups=mesh['batch'=8,'tensor'=4] {'batch'}, dimensions={0}, use_global_device_ids=true | all-gather | bytes 3456 | tf_op jit(solution)/shard_map/all_gather | solution.py:169
  54.0 31.0 %all_gather.28 = bf16[768,192]{1,0:T(8,128)(2,1)S(1)} all-gather(bf16[96,192]{1,0:T(8,128)(2,1)S(1)} %copy-done.50), channel_id=1, replica_groups=mesh['batch'=8,'tensor'=4] {'batch'}, dimensions={0}, use_global_device_ids=true | all-gather | bytes 331776 | tf_op jit(solution)/shard_map/all_gather | solution.py:163
  88.7 31.2 %all_gather.26 = bf16[768,192]{1,0:T(8,128)(2,1)S(1)} all-gather(bf16[96,192]{1,0:T(8,128)(2,1)S(1)} %copy-done.51), channel_id=1, replica_groups=mesh['batch'=8,'tensor'=4] {'batch'}, dimensions={0}, use_global_device_ids=true | all-gather | bytes 331776 | tf_op jit(solution)/shard_map/all_gather | solution.py:164
  125.1 31.3 %all_gather.29 = bf16[192,768]{0,1:T(8,128)(2,1)S(1)} all-gather(bf16[192,96]{0,1:T(8,128)(2,1)} %copy.70), channel_id=1, replica_groups=mesh['batch'=8,'tensor'=4] {'batch'}, dimensions={1}, use_global_device_ids=true | all-gather | bytes 331776 | tf_op jit(solution)/shard_map/all_gather | solution.py:165
  156.4 31.2 %all_gather.27 = bf16[768,192]{1,0:T(8,128)(2,1)S(1)} all-gather(bf16[96,192]{1,0:T(8,128)(2,1)} %param.29), channel_id=1, replica_groups=mesh['batch'=8,'tensor'=4] {'batch'}, dimensions={0}, use_global_device_ids=true | all-gather | bytes 331776 | tf_op jit(solution)/shard_map/all_gather | solution.py:162
  199.6 4.2 fusion.151
  206.3 3.2 fusion.4
  210.0 6.4 fusion.150
  222.0 90.3 %all-reduce.7.cloned.1.call-done = f32[1536,768]{1,0:T(8,128)} async-done(((f32[1536,768]{1,0:T(8,128)}), f32[1536,768]{1,0:T(8,128)}) %all-reduce.7.cloned.1.call-update) | async-done | bytes 4718608 | tf_op jit(solution)/shard_map/psum | solution.py:199
  319.5 6.2 fusion.203
  325.7 7.0 fusion.31
  334.2 4.2 fusion.204
  341.1 6.8 fusion.107
  347.9 5.9 all-to-all-start.5
  353.8 5.6 convolution_convert_fusion.5
  359.4 6.8 convolution_convert_fusion
  366.1 66.6 %all-reduce.9.cloned.1.call-done = f32[1536,768]{1,0:T(8,128)} async-done(((f32[1536,768]{1,0:T(8,128)}), f32[1536,768]{1,0:T(8,128)}) %all-reduce.9.cloned.1.call-update) | async-done | bytes 4718608 | tf_op jit(solution)/shard_map/psum | solution.py:214
  432.7 5.6 multiply_reduce_fusion.2
  438.6 4.3 multiply_add_fusion
  450.4 9.7 %fusion.128 = f32[512,3,64]{0,2,1:T(8,128)} fusion(bf16[512,3,64]{0,2,1:T(8,128)(2,1)} %bitcast.178, f32[3,512,512]{1,2,0:T(8,128)} %fusion.205, f32[3,512,512]{1,2,0:T(8,128)} %copy-done.18, f32[3,512]{1,0:T(4,128)S(1)} %copy-done.61, pred[512,512]{0,1:T(8,128)(4,1)} %copy-done.28), kind=kOutput, calls=%fused_computation.130 | convolution fusion | flops 114821120 | bytes 7149568 | tf_op jit(solution)/shard_map/while/body/eval_jaxpr/hqk,qhd->khd/dot_general | solution.py:132
  460.1 4.8 fusion.206
  465.0 5.1 fusion.207
  470.0 20.1 %fusion.145 = bf16[3,64,512]{2,1,0:T(8,128)(2,1)} fusion(bf16[1024,3,64]{0,2,1:T(8,128)(2,1)} %bitcast.171, f32[3,512,1024]{2,1,0:T(8,128)} %fusion.206, f32[3,512,1024]{2,1,0:T(8,128)} %copy-done.7, f32[3,512]{1,0:T(4,128)} %log_add_fusion.1, pred[512,1024]{1,0:T(8,128)(4,1)} %copy-done.23), kind=kOutput, calls=%fused_computation.139 | convolution fusion | flops 229739008 | bytes 13703168 | tf_op jit(solution)/shard_map/while/body/eval_jaxpr/hqk,khd->qhd/dot_general | solution.py:127
  493.5 9.8 %fusion.141 = bf16[3,64,512]{2,1,0:T(8,128)(2,1)} fusion(bf16[512,3,64]{0,2,1:T(8,128)(2,1)} %bitcast.179, f32[3,512,512]{1,2,0:T(8,128)} %fusion.205, f32[3,512,512]{1,2,0:T(8,128)} %copy-done.18, f32[3,512]{1,0:T(4,128)S(1)} %copy-done.61, pred[512,512]{0,1:T(8,128)(4,1)} %copy-done.28), kind=kOutput, calls=%fused_computation.137 | convolution fusion | flops 114919424 | bytes 6952960 | tf_op jit(solution)/shard_map/while/body/eval_jaxpr/hqk,khd->qhd/dot_general | solution.py:127
  503.3 26.8 %fusion.138 = bf16[3,64,512]{2,1,0:T(8,128)(2,1)} fusion(bf16[1536,3,64]{0,2,1:T(8,128)(2,1)S(1)} %bitcast.154, f32[3,512,1536]{2,1,0:T(8,128)} %fusion.207, f32[3,512,1536]{2,1,0:T(8,128)} %copy-done.6, f32[3,512]{1,0:T(4,128)S(1)} %copy-done.62, pred[512,1536]{1,0:T(8,128)(4,1)} %copy-done.16), kind=kOutput, calls=%fused_computation.136 | convolution fusion | flops 344558592 | bytes 20453376 | tf_op jit(solution)/shard_map/while/body/eval_jaxpr/hqk,khd->qhd/dot_general | solution.py:127
  530.0 20.4 %fusion.119 = f32[1536,3,64]{0,2,1:T(8,128)} fusion(f32[1536,3,64]{0,2,1:T(8,128)} %scatter-add.14, bf16[512,3,64]{0,2,1:T(8,128)(2,1)} %bitcast.176, f32[3,512,1024]{2,1,0:T(8,128)} %fusion.206, f32[3,512,1024]{2,1,0:T(8,128)} %copy-done.7, f32[3,512]{1,0:T(4,128)S(1)} %copy-done.63, pred[512,1024]{1,0:T(8,128)(4,1)} %copy-done.23), kind=kOutput, calls=%fused_computation.123 | convolution fusion | flops 229837312 | bytes 28000256 | tf_op jit(solution)/shard_map/while/body/eval_jaxpr/hqk,qhd->khd/dot_general | solution.py:132
  550.5 27.8 %fusion.76 = bf16[1536,3,64]{0,2,1:T(8,128)(2,1)} fusion(f32[1536,3,64]{0,2,1:T(8,128)} %fusion.119, bf16[512,3,64]{0,2,1:T(8,128)(2,1)S(1)} %bitcast.174, f32[3,512,1536]{2,1,0:T(8,128)} %fusion.207, f32[3,512,1536]{2,1,0:T(8,128)} %copy-done.6, f32[3,512]{1,0:T(4,128)S(1)} %copy-done.62, pred[512,1536]{1,0:T(8,128)(4,1)} %copy-done.16), kind=kOutput, calls=%fused_computation.94 | convolution fusion | flops 345050112 | bytes 21633024 | tf_op jit(solution)/shard_map/while/body/eval_jaxpr/hqk,qhd->khd/dot_general | solution.py:132
  578.2 4.1 fusion.208
  582.4 7.9 %fusion.125 = f32[1536,3,64]{0,2,1:T(8,128)} fusion(f32[1536,3,64]{0,2,1:T(8,128)} %scatter-add.16, bf16[512,3,64]{0,2,1:T(8,128)(2,1)S(1)} %bitcast.166, f32[3,512]{1,0:T(4,128)S(1)} %copy-done.63, pred[512,1024]{1,0:T(8,128)(4,1)S(1)} %copy-done.24, f32[3,512,1024]{2,1,0:T(8,128)} %copy-done.7), kind=kOutput, calls=%fused_computation.125 | convolution fusion | flops 212533248 | bytes 8591360 | tf_op jit(solution)/shard_map/while/body/eval_jaxpr/hqk,qhd->khd/dot_general | solution.py:140
  590.3 5.5 all-to-all-start.4
  598.2 8.8 %fusion.73 = bf16[1536,3,64]{0,2,1:T(8,128)(2,1)S(1)} fusion(f32[1536,3,64]{0,2,1:T(8,128)} %fusion.125, bf16[512,3,64]{0,2,1:T(8,128)(2,1)S(1)} %bitcast.160, f32[3,512]{1,0:T(4,128)S(1)} %copy-done.62, f32[3,512,1536]{2,1,0:T(8,128)} %copy-done.6, pred[512,1536]{1,0:T(8,128)(4,1)S(1)} %copy-done.17), kind=kOutput, calls=%fused_computation.93 | convolution fusion | flops 319094784 | bytes 12195840 | tf_op jit(solution)/shard_map/while/body/eval_jaxpr/hqk,qhd->khd/dot_general | solution.py:140
  616.4 7.8 %all-to-all-done.4 = bf16[8,96,768]{2,1,0:T(8,128)(2,1)} async-done(((bf16[8,96,768]{2,1,0:T(8,128)(2,1)}), bf16[8,96,768]{2,1,0:T(8,128)(2,1)}, u32[]{:S(2)}, u32[]{:S(2)}) %all-to-all-start.4) | async-done | bytes 1179680 | tf_op jit(solution)/shard_map/all_to_all | solution.py:18
  624.3 3.6 all-to-all-start.2
  627.9 3.4 convolution_convert_fusion.8
  635.2 4.5 all-to-all-done.2
  639.7 4.1 all-to-all-start
  644.4 3.2 convolution_convert_fusion.7
  651.6 3.7 all-to-all-done
  655.3 4.1 all-to-all-start.1
  661.6 3.9 convolution_convert_fusion.9
  670.1 3.7 all-to-all-start.3
  685.7 19.5 %all-reduce.11.cloned.1.call-done = (bf16[1536,768]{1,0:T(8,128)(2,1)}, bf16[1536,768]{1,0:T(8,128)(2,1)}) async-done(((bf16[1536,768]{1,0:T(8,128)(2,1)}, bf16[1536,768]{1,0:T(8,128)(2,1)}), (bf16[1536,768]{1,0:T(8,128)(2,1)}, bf16[1536,768]{1,0:T(8,128)(2,1)})) %all-reduce.11.cloned.1.call-update) | async-done | bytes 4718608 | tf_op jit(solution)/shard_map/psum | solution.py:206
  705.2 3.8 fusion.24
  711.7 5.5 all-to-all-start.7
  717.4 5.2 multiply_convert_fusion.4
  726.3 6.0 all-to-all-start.6
  732.9 5.9 all-to-all-done.6
  (251 shorter events, 104.7 us)
Async XLA Ops:
  8.0 77.0 %copy-start.1 = (bf16[1536,768]{1,0:T(8,128)(2,1)S(1)}, bf16[1536,768]{1,0:T(8,128)(2,1)}, u32[]{:S(2)}) copy-start(bf16[1536,768]{1,0:T(8,128)(2,1)} %param.27) | copy-start | bytes 7077892
  8.0 45.9 %copy-start.50 = (bf16[96,192]{1,0:T(8,128)(2,1)S(1)}, bf16[96,192]{1,0:T(8,128)(2,1)}, u32[]{:S(2)}) copy-start(bf16[96,192]{1,0:T(8,128)(2,1)} %param.30) | copy-start | bytes 110596
  8.0 304.2 %all-reduce.7.cloned.1.call-start = ((), (), s32[]{:S(2)}) async-start(), calls=%async_computation.8 | async-start | bytes 9437184 | tf_op jit(solution)/shard_map/psum | solution.py:199
  32.3 53.9 %copy-start.46 = (f32[768]{0:T(1024)}, f32[768]{0:T(1024)S(1)}, u32[]{:S(2)}) copy-start(f32[768]{0:T(1024)S(1)} %get-tuple-element.217) | copy-start | bytes 9220
  51.4 35.7 %copy-start.37 = (f32[1536]{0:T(1024)}, f32[1536]{0:T(1024)S(1)}, u32[]{:S(2)}) copy-start(f32[1536]{0:T(1024)S(1)} %broadcast_multiply_fusion.5) | copy-start | bytes 18436
  53.9 31.0 %copy-start.44 = (f32[1536]{0:T(1024)}, f32[1536]{0:T(1024)S(1)}, u32[]{:S(2)}) copy-start(f32[1536]{0:T(1024)S(1)} %add_rsqrt_fusion.1) | copy-start | bytes 18436
  86.2 36.1 %copy-start.3 = (bf16[1536,768]{1,0:T(8,128)(2,1)}, bf16[1536,768]{1,0:T(8,128)(2,1)S(1)}, u32[]{:S(2)}) copy-start(bf16[1536,768]{1,0:T(8,128)(2,1)S(1)} %fusion.17) | copy-start | bytes 7077892
  87.1 116.7 %copy-start.21 = (bf16[1536,192]{0,1:T(8,128)(2,1)}, bf16[1536,192]{0,1:T(8,128)(2,1)S(1)}, u32[]{:S(2)}) copy-start(bf16[1536,192]{0,1:T(8,128)(2,1)S(1)} %convolution_convert_fusion.2) | copy-start | bytes 1769476
  125.1 66.2 %copy-start.43 = (bf16[512,192]{0,1:T(8,128)(2,1)S(1)}, bf16[512,192]{0,1:T(8,128)(2,1)}, u32[]{:S(2)}) copy-start(bf16[512,192]{0,1:T(8,128)(2,1)} %slice.337) | copy-start | bytes 589828
  156.4 60.1 %copy-start.14 = (bf16[192,768]{0,1:T(8,128)(2,1)}, bf16[192,768]{0,1:T(8,128)(2,1)S(1)}, u32[]{:S(2)}) copy-start(bf16[192,768]{0,1:T(8,128)(2,1)S(1)} %all_gather.29) | copy-start | bytes 884740
  190.4 13.4 %copy-start.39 = (bf16[512,192]{0,1:T(8,128)(2,1)}, bf16[512,192]{0,1:T(8,128)(2,1)S(1)}, u32[]{:S(2)}) copy-start(bf16[512,192]{0,1:T(8,128)(2,1)S(1)} %get-tuple-element.228) | copy-start | bytes 589828
  191.2 18.3 %copy-start.16 = (pred[512,1536]{1,0:T(8,128)(4,1)}, pred[512,1536]{1,0:T(8,128)(4,1)S(1)}, u32[]{:S(2)}) copy-start(pred[512,1536]{1,0:T(8,128)(4,1)S(1)} %fusion.50) | copy-start | bytes 2359300
  197.4 6.4 copy-start.7
  197.4 6.4 copy-start.52
  209.6 6.9 copy-start.55
  219.5 100.0 %all-gather.5.cloned.1.call-start = ((), (), s32[]{:S(2)}) async-start(), calls=%async_computation.9 | async-start | bytes 1327104 | tf_op jit(solution)/shard_map/all_gather | solution.py:166
  220.1 105.6 %all-gather.7.cloned.1.call-start = ((), (), s32[]{:S(2)}) async-start(), calls=%async_computation.10 | async-start | bytes 1327104 | tf_op jit(solution)/shard_map/all_gather | solution.py:167
  220.7 212.0 %all-reduce.9.cloned.1.call-start = ((), (), s32[]{:S(2)}) async-start(), calls=%async_computation.11 | async-start | bytes 9437184 | tf_op jit(solution)/shard_map/psum | solution.py:214
  325.7 8.5 %copy-start.66 = (bf16[768,768]{1,0:T(8,128)(2,1)S(1)}, bf16[768,768]{1,0:T(8,128)(2,1)}, u32[]{:S(2)}) copy-start(bf16[768,768]{1,0:T(8,128)(2,1)} %all-gather.5.cloned.1.call-done) | copy-start | bytes 3538948
  347.9 242.4 %all-to-all-start.5 = ((bf16[8,768,96]{1,2,0:T(8,128)(2,1)}), bf16[8,768,96]{1,2,0:T(8,128)(2,1)}, u32[]{:S(2)}, u32[]{:S(2)}) async-start(bf16[8,768,96]{1,2,0:T(8,128)(2,1)} %bitcast.158), calls=%async_computation.5 | async-start | bytes 2359296 | tf_op jit(solution)/shard_map/all_to_all | solution.py:18
  353.8 5.6 copy-start.65
  432.7 5.6 copy-start.5
  432.7 5.9 copy-start.20
  432.7 5.9 copy-start.49
  432.7 5.9 copy-start.58
  470.0 22.3 %copy-start.36 = (f32[512,3,64]{0,2,1:T(8,128)S(1)}, f32[512,3,64]{0,2,1:T(8,128)}, u32[]{:S(2)}) copy-start(f32[512,3,64]{0,2,1:T(8,128)} %fusion.128) | copy-start | bytes 1179652
  493.5 9.8 %copy-start.22 = (bf16[1536,192]{0,1:T(8,128)(2,1)S(1)}, bf16[1536,192]{0,1:T(8,128)(2,1)}, u32[]{:S(2)}) copy-start(bf16[1536,192]{0,1:T(8,128)(2,1)} %copy-done.21) | copy-start | bytes 1769476
  493.5 9.8 %copy-start.62 = (f32[3,512]{1,0:T(4,128)S(1)}, f32[3,512]{1,0:T(4,128)}, u32[]{:S(2)}) copy-start(f32[3,512]{1,0:T(4,128)} %log_add_fusion) | copy-start | bytes 18436
  503.2 26.8 %copy-start.63 = (f32[3,512]{1,0:T(4,128)S(1)}, f32[3,512]{1,0:T(4,128)}, u32[]{:S(2)}) copy-start(f32[3,512]{1,0:T(4,128)} %log_add_fusion.1) | copy-start | bytes 18436
  530.0 20.4 %copy-start.40 = (bf16[512,192]{0,1:T(8,128)(2,1)S(1)}, bf16[512,192]{0,1:T(8,128)(2,1)}, u32[]{:S(2)}) copy-start(bf16[512,192]{0,1:T(8,128)(2,1)} %copy-done.39) | copy-start | bytes 589828
  550.5 27.8 %copy-start.13 = (bf16[768,192]{1,0:T(8,128)(2,1)S(1)}, bf16[768,192]{1,0:T(8,128)(2,1)}, u32[]{:S(2)}) copy-start(bf16[768,192]{1,0:T(8,128)(2,1)} %copy-done.12) | copy-start | bytes 884740
  582.4 13.7 %copy-start.11 = (bf16[768,192]{1,0:T(8,128)(2,1)S(1)}, bf16[768,192]{1,0:T(8,128)(2,1)}, u32[]{:S(2)}) copy-start(bf16[768,192]{1,0:T(8,128)(2,1)} %copy-done.10) | copy-start | bytes 884740
  590.3 34.0 %all-to-all-start.4 = ((bf16[8,96,768]{2,1,0:T(8,128)(2,1)}), bf16[8,96,768]{2,1,0:T(8,128)(2,1)}, u32[]{:S(2)}, u32[]{:S(2)}) async-start(bf16[8,96,768]{2,1,0:T(8,128)(2,1)} %bitcast.157), calls=%async_computation.4 | async-start | bytes 2359296 | tf_op jit(solution)/shard_map/all_to_all | solution.py:18
  595.8 109.4 %all-reduce.11.cloned.1.call-start = ((), (), s32[]{:S(2)}) async-start(), calls=%async_computation.12 | async-start | bytes 9437184 | tf_op jit(solution)/shard_map/psum | solution.py:206
  596.1 11.8 %slice-start.2 = ((s8[4718592]{0:T(1024)(128)(4,1)}), s8[4194304]{0:T(1024)(128)(4,1)S(1)}, s32[]{:S(2)}) async-start(s8[4718592]{0:T(1024)(128)(4,1)} %bitcast.147), calls=%async_computation.15 | async-start | bytes 8388608
  598.2 9.6 %slice-start.3 = ((s8[4718592]{0:T(1024)(128)(4,1)}), s8[524288]{0:T(1024)(128)(4,1)S(1)}, s32[]{:S(2)}) async-start(s8[4718592]{0:T(1024)(128)(4,1)} %bitcast.147), calls=%async_computation.16 | async-start | bytes 1048576
  598.2 9.6 %copy-start.9 = (bf16[768,192]{1,0:T(8,128)(2,1)S(1)}, bf16[768,192]{1,0:T(8,128)(2,1)}, u32[]{:S(2)}) copy-start(bf16[768,192]{1,0:T(8,128)(2,1)} %copy-done.8) | copy-start | bytes 884740
  624.3 15.5 %all-to-all-start.2 = ((bf16[8,96,192]{1,2,0:T(8,128)(2,1)}), bf16[8,96,192]{1,2,0:T(8,128)(2,1)S(1)}, u32[]{:S(2)}, u32[]{:S(2)}) async-start(bf16[8,96,192]{1,2,0:T(8,128)(2,1)} %copy.78), calls=%async_computation.2 | async-start | bytes 786432 | tf_op jit(solution)/shard_map/all_to_all | solution.py:18
  639.7 15.6 %all-to-all-start = ((bf16[8,96,192]{1,2,0:T(8,128)(2,1)}), bf16[8,96,192]{1,2,0:T(8,128)(2,1)}, u32[]{:S(2)}, u32[]{:S(2)}) async-start(bf16[8,96,192]{1,2,0:T(8,128)(2,1)} %copy.74), calls=%async_computation | async-start | bytes 786432 | tf_op jit(solution)/shard_map/all_to_all | solution.py:18
  655.3 14.8 %all-to-all-start.1 = ((bf16[8,96,192]{1,2,0:T(8,128)(2,1)}), bf16[8,96,192]{1,2,0:T(8,128)(2,1)}, u32[]{:S(2)}, u32[]{:S(2)}) async-start(bf16[8,96,192]{1,2,0:T(8,128)(2,1)} %copy.76), calls=%async_computation.1 | async-start | bytes 786432 | tf_op jit(solution)/shard_map/all_to_all | solution.py:18
  661.6 43.6 %copy-start.38 = (f32[1536]{0:T(1024)S(1)}, f32[1536]{0:T(1024)}, u32[]{:S(2)}) copy-start(f32[1536]{0:T(1024)} %copy-done.37) | copy-start | bytes 18436
  661.6 43.6 %copy-start.45 = (f32[1536]{0:T(1024)S(1)}, f32[1536]{0:T(1024)}, u32[]{:S(2)}) copy-start(f32[1536]{0:T(1024)} %copy-done.44) | copy-start | bytes 18436
  665.5 39.7 %copy-start.47 = (f32[768]{0:T(1024)S(1)}, f32[768]{0:T(1024)}, u32[]{:S(2)}) copy-start(f32[768]{0:T(1024)} %copy-done.46) | copy-start | bytes 9220
  670.1 14.8 %all-to-all-start.3 = ((bf16[8,192,96]{2,1,0:T(8,128)(2,1)}), bf16[8,192,96]{2,1,0:T(8,128)(2,1)S(1)}, u32[]{:S(2)}, u32[]{:S(2)}) async-start(bf16[8,192,96]{2,1,0:T(8,128)(2,1)} %bitcast.139), calls=%async_computation.3 | async-start | bytes 786432 | tf_op jit(solution)/shard_map/all_to_all | solution.py:18
  677.7 39.7 %copy-start.56 = (f32[1536]{0:T(1024)S(1)}, f32[1536]{0:T(1024)}, u32[]{:S(2)}) copy-start(f32[1536]{0:T(1024)} %fusion.154) | copy-start | bytes 18436
  705.2 17.4 %slice-start = ((s8[4718592]{0:T(1024)(128)(4,1)}), s8[524288]{0:T(1024)(128)(4,1)S(1)}, s32[]{:S(2)}) async-start(s8[4718592]{0:T(1024)(128)(4,1)} %bitcast.145), calls=%async_computation.13 | async-start | bytes 1048576
  711.7 14.6 %all-to-all-start.7 = ((bf16[8,2,96]{2,1,0:T(2,128)(2,1)}), bf16[8,2,96]{2,1,0:T(2,128)(2,1)S(1)}, u32[]{:S(2)}, u32[]{:S(2)}) async-start(bf16[8,2,96]{2,1,0:T(2,128)(2,1)} %copy.82), calls=%async_computation.7 | async-start | bytes 8192 | tf_op jit(solution)/shard_map/all_to_all | solution.py:18
  726.3 12.5 %all-to-all-start.6 = ((bf16[8,2,96]{2,1,0:T(2,128)(2,1)}), bf16[8,2,96]{2,1,0:T(2,128)(2,1)S(1)}, u32[]{:S(2)}, u32[]{:S(2)}) async-start(bf16[8,2,96]{2,1,0:T(2,128)(2,1)} %copy.81), calls=%async_computation.6 | async-start | bytes 8192 | tf_op jit(solution)/shard_map/all_to_all | solution.py:18
  (37 other events, 120.4 us)
Sparse Core Ops, SparseCore 0:
  219.7 92.5 all-reduce.6
  338.5 94.1 all-reduce.8
  610.3 94.8 all-reduce.10
Sparse Core Ops, SparseCore 1:
  222.2 39.9 all-gather.4
  264.2 40.0 all-gather.6
where the time goes:
time: 757 us; the launch traced here: 747 us
  matrix products  231 us (31%)
  waiting for transfers between devices  205 us (27%)
  blocking collectives  163 us (22%)
  other arithmetic  57.6 us (8%)
  starting transfers between devices  38.8 us (5%)
  local copies, waits for them, and re-layouts  34.2 us (5%)
  between operations  17.1 us (2%)
    psum x1, waiting for transfers between devices, per_device(): hidden = inputs + lax.psum(attn_partial, 'tensor')  90.3 us
    psum x1, waiting for transfers between devices, per_device(): grad_normed_two = lax.psum(mid_partial, 'tensor')  66.6 us
    dot_general x3, matrix products, attend_back(): jnp.einsum('hqk,qhd->khd', grad_raw, queries[begin_row:end_row], preferre...  57.9 us
    dot_general x3, matrix products, attend_back(): jnp.einsum('hqk,khd->qhd', grad_raw, key_rows[:end_row], preferred_elemen...  56.7 us
    all_to_all x8, starting transfers between devices, summed_on_arrival(): lax.all_to_all(cut_along(value, dim, length), axis, 0, 0, tiled=True)  38.4 us
    all_gather x1, blocking collectives, per_device(): lax.all_gather(w_out, 'batch', axis=1, tiled=True)  31.3 us
    all_gather x1, blocking collectives, per_device(): lax.all_gather(w_value, 'batch', axis=0, tiled=True)  31.2 us
    all_gather x1, blocking collectives, per_device(): lax.all_gather(w_query, 'batch', axis=0, tiled=True)  31.2 us
  transfers between devices with their start and end apart: 13, of which 9 were waited for; matrix products, arithmetic and copies ran while one was open for 34% of the time, Pallas kernels for 0%

commit v1 on v0

--- a/solution.py
+++ b/solution.py
@@ -5,6 +5,28 @@
 
 HD = 64
 epsilon = 1e-05
+
+
+def laid_out(blocks, dim):
+    lengths = list(blocks.shape[1:])
+    lengths[dim] *= blocks.shape[0]
+    return jnp.moveaxis(blocks, 0, dim).reshape(lengths)
+
+
+def ring_gather(value, axis, dim):
+    peers = lax.axis_size(axis)
+    pairs = [(i, (i + 1) % peers) for i in range(peers)]
+    back = [(b, a) for a, b in pairs]
+    lower, upper = ([], [])
+    for step in range(peers - 1):
+        if step % 2 == 0:
+            lower.append(lax.ppermute(lower[-1] if lower else value, axis, pairs))
+        else:
+            upper.append(lax.ppermute(upper[-1] if upper else value, axis, back))
+    blocks = jnp.stack([*lower[::-1], value, *upper])
+    shift = lax.axis_index(axis) - len(lower)
+    blocks = blocks[(jnp.arange(peers) - shift) % peers]
+    return laid_out(blocks, dim)
 
 
 def cut_along(value, dim, length):
@@ -159,7 +181,7 @@
     block_rows = min(512, seq_len)
     scaling = float(HD) ** (-0.5)
     gathered = (
-        lax.all_gather(w_query, "batch", axis=0, tiled=True),
+        ring_gather(w_query, "batch", 0),
         lax.all_gather(w_key, "batch", axis=0, tiled=True),
         lax.all_gather(w_value, "batch", axis=0, tiled=True),
         lax.all_gather(w_out, "batch", axis=1, tiled=True),

time: 757 us -> 742 us (0.980)
  blocking collectives: 163 us -> 130 us
  starting transfers between devices: 38.8 us -> 56.8 us
  local copies, waits for them, and re-layouts: 34.2 us -> 45.2 us
  matrix products: 231 us -> 222 us
    all_gather x1 -> x0, blocking collectives: 31.2 us -> none  [per_device(): lax.all_gather(w_query, 'batch', axis=0, tiled=True)]
    ppermute x0 -> x7, starting transfers between devices: none -> 15.8 us  [the longest x3 10.9 us: ring_gather(): upper.append(lax.ppermute(upper[-1] if upper else value, axis, back))]
    all_to_all x8, waiting for transfers between devices: 27.2 us -> 18 us  [summed_on_arrival(): lax.all_to_all(cut_along(value, dim, length), axis, 0, 0, tiled=True)]
    unnamed x148 -> x155, local copies, waits for them, and re-layouts: 10.3 us -> 18.2 us
  transfers between devices with their start and end apart: 13 -> 20, of which waited for: 9 -> 9; matrix products, arithmetic and copies ran while one was open for 34% -> 37% of each run, Pallas kernels for 0% -> 0%
where the time goes in v1:
time: 742 us; the launch traced here: 735 us
  matrix products  222 us (30%)
  waiting for transfers between devices  203 us (27%)
  blocking collectives  130 us (18%)
  other arithmetic  60.2 us (8%)
  starting transfers between devices  56.8 us (8%)
  local copies, waits for them, and re-layouts  45.2 us (6%)
  between operations  17.2 us (2%)
    psum x1, waiting for transfers between devices, per_device(): hidden = inputs + lax.psum(attn_partial, 'tensor')  89.1 us
    psum x1, waiting for transfers between devices, per_device(): grad_normed_two = lax.psum(mid_partial, 'tensor')  66.8 us
    dot_general x3, matrix products, attend_back(): jnp.einsum('hqk,qhd->khd', grad_raw, queries[begin_row:end_row], preferre...  54.3 us
    dot_general x3, matrix products, attend_back(): jnp.einsum('hqk,khd->qhd', grad_raw, key_rows[:end_row], preferred_elemen...  52.7 us
    all_to_all x8, starting transfers between devices, summed_on_arrival(): lax.all_to_all(cut_along(value, dim, length), axis, 0, 0, tiled=True)  40.8 us
    all_gather x1, blocking collectives, per_device(): lax.all_gather(w_out, 'batch', axis=1, tiled=True)  33.3 us
    all_gather x1, blocking collectives, per_device(): lax.all_gather(w_value, 'batch', axis=0, tiled=True)  31.1 us
    all_gather x1, blocking collectives, per_device(): lax.all_gather(w_key, 'batch', axis=0, tiled=True)  31 us
  transfers between devices with their start and end apart: 20, of which 9 were waited for; matrix products, arithmetic and copies ran while one was open for 37% of the time, Pallas kernels for 0%

profile of v1, /device:TPU:0, one launch (start us, length us, event | category | flops | bytes accessed | tf_op | source)
XLA Modules:
  0.0 735.1 jit_solution(12993207171623276223)
XLA Ops:
  8.1 3.0 collective-permute-start
  11.1 3.1 collective-permute-start.4
  16.5 18.3 %all-gather = bf16[8,96,2]{1,2,0:T(2,128)(2,1)S(1)} all-gather(bf16[1,96,2]{1,2,0:T(2,128)(2,1)} %bitcast.208), channel_id=1, replica_groups=mesh['batch'=8,'tensor'=4] {'batch'}, dimensions={0}, use_global_device_ids=true | all-gather | bytes 3456 | tf_op jit(solution)/shard_map/all_gather | solution.py:190
  35.5 16.4 %all-gather.1 = bf16[8,96,2]{1,2,0:T(2,128)(2,1)S(1)} all-gather(bf16[1,96,2]{1,2,0:T(2,128)(2,1)} %bitcast.209), channel_id=1, replica_groups=mesh['batch'=8,'tensor'=4] {'batch'}, dimensions={0}, use_global_device_ids=true | all-gather | bytes 3456 | tf_op jit(solution)/shard_map/all_gather | solution.py:191
  57.2 31.0 %all_gather.24 = bf16[768,192]{1,0:T(8,128)(2,1)S(1)} all-gather(bf16[96,192]{1,0:T(8,128)(2,1)S(1)} %copy-done.52), channel_id=1, replica_groups=mesh['batch'=8,'tensor'=4] {'batch'}, dimensions={0}, use_global_device_ids=true | all-gather | bytes 331776 | tf_op jit(solution)/shard_map/all_gather | solution.py:185
  88.1 31.1 %all_gather.23 = bf16[768,192]{1,0:T(8,128)(2,1)S(1)} all-gather(bf16[96,192]{1,0:T(8,128)(2,1)S(1)} %copy-done.53), channel_id=1, replica_groups=mesh['batch'=8,'tensor'=4] {'batch'}, dimensions={0}, use_global_device_ids=true | all-gather | bytes 331776 | tf_op jit(solution)/shard_map/all_gather | solution.py:186
  127.9 33.3 %all_gather.25 = bf16[192,768]{0,1:T(8,128)(2,1)} all-gather(bf16[192,96]{0,1:T(8,128)(2,1)} %copy.70), channel_id=1, replica_groups=mesh['batch'=8,'tensor'=4] {'batch'}, dimensions={1}, use_global_device_ids=true | all-gather | bytes 331776 | tf_op jit(solution)/shard_map/all_gather | solution.py:187
  171.3 4.9 collective-permute-start.6
  198.3 4.2 fusion.151
  205.2 3.2 fusion.4
  208.8 6.4 fusion.150
  220.8 89.1 %all-reduce.7.cloned.1.call-done = f32[1536,768]{1,0:T(8,128)} async-done(((f32[1536,768]{1,0:T(8,128)}), f32[1536,768]{1,0:T(8,128)}) %all-reduce.7.cloned.1.call-update) | async-done | bytes 4718608 | tf_op jit(solution)/shard_map/psum | solution.py:221
  317.4 6.2 fusion.204
  323.6 7.0 fusion.31
  332.1 4.2 fusion.205
  339.0 6.8 fusion.107
  345.8 5.7 all-to-all-start.5
  351.5 5.6 convolution_convert_fusion.5
  357.1 6.8 convolution_convert_fusion
  363.9 66.8 %all-reduce.9.cloned.1.call-done = f32[1536,768]{1,0:T(8,128)} async-done(((f32[1536,768]{1,0:T(8,128)}), f32[1536,768]{1,0:T(8,128)}) %all-reduce.9.cloned.1.call-update) | async-done | bytes 4718608 | tf_op jit(solution)/shard_map/psum | solution.py:236
  430.7 5.6 multiply_reduce_fusion.2
  436.5 4.4 multiply_add_fusion
  448.4 9.8 %fusion.128 = f32[512,3,64]{0,2,1:T(8,128)} fusion(bf16[512,3,64]{0,2,1:T(8,128)(2,1)} %bitcast.197, f32[3,512,512]{1,2,0:T(8,128)} %fusion.206, f32[3,512,512]{1,2,0:T(8,128)} %copy-done.18, f32[3,512]{1,0:T(4,128)S(1)} %copy-done.62, pred[512,512]{0,1:T(8,128)(4,1)} %compare_and_fusion.1), kind=kOutput, calls=%fused_computation.131 | convolution fusion | flops 114821120 | bytes 7149568 | tf_op jit(solution)/shard_map/while/body/eval_jaxpr/hqk,qhd->khd/dot_general | solution.py:154
  462.4 4.8 fusion.207
  467.3 5.1 fusion.208
  472.4 26.9 %fusion.138 = bf16[3,64,512]{2,1,0:T(8,128)(2,1)} fusion(bf16[1536,3,64]{0,2,1:T(8,128)(2,1)} %bitcast.172, f32[3,512,1536]{2,1,0:T(8,128)} %fusion.208, f32[3,512,1536]{2,1,0:T(8,128)} %copy-done.6, f32[3,512]{1,0:T(4,128)S(1)} %copy-done.63, pred[512,1536]{1,0:T(8,128)(4,1)} %fusion.50), kind=kOutput, calls=%fused_computation.137 | convolution fusion | flops 344558592 | bytes 20453376 | tf_op jit(solution)/shard_map/while/body/eval_jaxpr/hqk,khd->qhd/dot_general | solution.py:149
  499.2 16.1 %fusion.145 = bf16[3,64,512]{2,1,0:T(8,128)(2,1)} fusion(bf16[1024,3,64]{0,2,1:T(8,128)(2,1)} %bitcast.190, f32[3,512,1024]{2,1,0:T(8,128)} %fusion.207, f32[3,512,1024]{2,1,0:T(8,128)} %copy-done.7, f32[3,512]{1,0:T(4,128)S(1)} %copy-done.64, pred[512,1024]{1,0:T(8,128)(4,1)S(1)} %copy-done.24), kind=kOutput, calls=%fused_computation.140 | convolution fusion | flops 229739008 | bytes 13703168 | tf_op jit(solution)/shard_map/while/body/eval_jaxpr/hqk,khd->qhd/dot_general | solution.py:149
  515.3 16.8 %fusion.119 = f32[1536,3,64]{0,2,1:T(8,128)} fusion(f32[1536,3,64]{0,2,1:T(8,128)} %scatter-add.14, bf16[512,3,64]{0,2,1:T(8,128)(2,1)} %bitcast.195, f32[3,512,1024]{2,1,0:T(8,128)} %fusion.207, f32[3,512,1024]{2,1,0:T(8,128)} %copy-done.7, f32[3,512]{1,0:T(4,128)S(1)} %copy-done.64, pred[512,1024]{1,0:T(8,128)(4,1)S(1)} %copy-done.24), kind=kOutput, calls=%fused_computation.124 | convolution fusion | flops 229837312 | bytes 28000256 | tf_op jit(solution)/shard_map/while/body/eval_jaxpr/hqk,qhd->khd/dot_general | solution.py:154
  532.2 8.0 %fusion.125 = f32[1536,3,64]{0,2,1:T(8,128)} fusion(f32[1536,3,64]{0,2,1:T(8,128)} %scatter-add.16, bf16[512,3,64]{0,2,1:T(8,128)(2,1)} %bitcast.185, f32[3,512]{1,0:T(4,128)S(1)} %copy-done.64, pred[512,1024]{1,0:T(8,128)(4,1)S(1)} %copy-done.24, f32[3,512,1024]{2,1,0:T(8,128)} %copy-done.7), kind=kOutput, calls=%fused_computation.126 | convolution fusion | flops 212533248 | bytes 8591360 | tf_op jit(solution)/shard_map/while/body/eval_jaxpr/hqk,qhd->khd/dot_general | solution.py:162
  540.2 9.7 %fusion.73 = bf16[1536,3,64]{0,2,1:T(8,128)(2,1)} fusion(f32[1536,3,64]{0,2,1:T(8,128)} %fusion.125, bf16[512,3,64]{0,2,1:T(8,128)(2,1)S(1)} %bitcast.179, f32[3,512]{1,0:T(4,128)S(1)} %copy-done.63, f32[3,512,1536]{2,1,0:T(8,128)} %copy-done.6, pred[512,1536]{1,0:T(8,128)(4,1)S(1)} %copy-done.17), kind=kOutput, calls=%fused_computation.94 | convolution fusion | flops 319094784 | bytes 12195840 | tf_op jit(solution)/shard_map/while/body/eval_jaxpr/hqk,qhd->khd/dot_general | solution.py:162
  549.9 5.5 all-to-all-start.4
  555.5 9.7 %fusion.141 = bf16[3,64,512]{2,1,0:T(8,128)(2,1)} fusion(bf16[512,3,64]{0,2,1:T(8,128)(2,1)S(1)} %bitcast.199, f32[3,512,512]{1,2,0:T(8,128)} %fusion.206, f32[3,512,512]{1,2,0:T(8,128)} %copy-done.18, f32[3,512]{1,0:T(4,128)S(1)} %copy-done.62, pred[512,512]{0,1:T(8,128)(4,1)} %compare_and_fusion.1), kind=kOutput, calls=%fused_computation.138 | convolution fusion | flops 114919424 | bytes 6952960 | tf_op jit(solution)/shard_map/while/body/eval_jaxpr/hqk,khd->qhd/dot_general | solution.py:149
  565.1 27.8 %fusion.76 = bf16[1536,3,64]{0,2,1:T(8,128)(2,1)} fusion(f32[1536,3,64]{0,2,1:T(8,128)} %fusion.119, bf16[512,3,64]{0,2,1:T(8,128)(2,1)S(1)} %bitcast.193, f32[3,512,1536]{2,1,0:T(8,128)} %fusion.208, f32[3,512,1536]{2,1,0:T(8,128)} %copy-done.6, f32[3,512]{1,0:T(4,128)S(1)} %copy-done.63, pred[512,1536]{1,0:T(8,128)(4,1)} %fusion.50), kind=kOutput, calls=%fused_computation.95 | convolution fusion | flops 345050112 | bytes 21633024 | tf_op jit(solution)/shard_map/while/body/eval_jaxpr/hqk,qhd->khd/dot_general | solution.py:154
  599.3 3.0 convolution_convert_fusion.6
  604.5 5.9 all-to-all-start.2
  610.5 3.4 convolution_convert_fusion.8
  617.9 3.6 all-to-all-done.2
  621.4 4.4 all-to-all-start
  626.4 3.3 convolution_convert_fusion.7
  636.6 4.1 all-to-all-start.1
  642.9 3.7 convolution_convert_fusion.9
  651.5 3.7 all-to-all-start.3
  667.0 26.2 %all-reduce.11.cloned.1.call-done = (bf16[1536,768]{1,0:T(8,128)(2,1)}, bf16[1536,768]{1,0:T(8,128)(2,1)}) async-done(((bf16[1536,768]{1,0:T(8,128)(2,1)}, bf16[1536,768]{1,0:T(8,128)(2,1)}), (bf16[1536,768]{1,0:T(8,128)(2,1)}, bf16[1536,768]{1,0:T(8,128)(2,1)})) %all-reduce.11.cloned.1.call-update) | async-done | bytes 4718608 | tf_op jit(solution)/shard_map/psum | solution.py:228
  693.2 3.8 fusion.24
  699.8 5.5 all-to-all-start.7
  705.4 5.2 multiply_convert_fusion.4
  714.4 6.0 all-to-all-start.6
  721.0 5.9 all-to-all-done.6
  (274 shorter events, 127.0 us)
Async XLA Ops:
  8.0 111.2 %copy-start.1 = (bf16[1536,768]{1,0:T(8,128)(2,1)S(1)}, bf16[1536,768]{1,0:T(8,128)(2,1)}, u32[]{:S(2)}) copy-start(bf16[1536,768]{1,0:T(8,128)(2,1)} %param.27) | copy-start | bytes 7077892
  8.0 49.1 %copy-start.52 = (bf16[96,192]{1,0:T(8,128)(2,1)S(1)}, bf16[96,192]{1,0:T(8,128)(2,1)}, u32[]{:S(2)}) copy-start(bf16[96,192]{1,0:T(8,128)(2,1)} %param.30) | copy-start | bytes 110596
  8.0 80.1 %copy-start.53 = (bf16[96,192]{1,0:T(8,128)(2,1)S(1)}, bf16[96,192]{1,0:T(8,128)(2,1)}, u32[]{:S(2)}) copy-start(bf16[96,192]{1,0:T(8,128)(2,1)} %param.31) | copy-start | bytes 110596
  8.0 301.9 %all-reduce.7.cloned.1.call-start = ((), (), s32[]{:S(2)}) async-start(), calls=%async_computation.8 | async-start | bytes 9437184 | tf_op jit(solution)/shard_map/psum | solution.py:221
  8.1 119.8 %collective-permute-start = (bf16[96,192]{1,0:T(8,128)(2,1)}, bf16[96,192]{1,0:T(8,128)(2,1)}, u32[]{:S(2)}, u32[]{:S(2)}) collective-permute-start(bf16[96,192]{1,0:T(8,128)(2,1)} %param.29), channel_id=1, source_target_pairs={{0,4},{4,8},{8,12},{12,16},{16,20},{20,24},{24,28},{28,0},{1,5},{5... | collective-permute-start | bytes 110600 | tf_op jit(solution)/shard_map/ppermute | solution.py:23
  11.1 152.0 %collective-permute-start.4 = (bf16[96,192]{1,0:T(8,128)(2,1)}, bf16[96,192]{1,0:T(8,128)(2,1)}, u32[]{:S(2)}, u32[]{:S(2)}) collective-permute-start(bf16[96,192]{1,0:T(8,128)(2,1)} %param.29), channel_id=1, source_target_pairs={{4,0},{8,4},{12,8},{16,12},{20,16},{24,20},{28,24},{0,28},{5,1},{9... | collective-permute-start | bytes 110600 | tf_op jit(solution)/shard_map/ppermute | solution.py:25
  35.5 84.9 %copy-start.48 = (f32[768]{0:T(1024)}, f32[768]{0:T(1024)S(1)}, u32[]{:S(2)}) copy-start(f32[768]{0:T(1024)S(1)} %get-tuple-element.217) | copy-start | bytes 9220
  54.6 66.8 %copy-start.35 = (f32[1536]{0:T(1024)}, f32[1536]{0:T(1024)S(1)}, u32[]{:S(2)}) copy-start(f32[1536]{0:T(1024)S(1)} %broadcast_multiply_fusion.5) | copy-start | bytes 18436
  57.2 62.0 %copy-start.46 = (f32[1536]{0:T(1024)}, f32[1536]{0:T(1024)S(1)}, u32[]{:S(2)}) copy-start(f32[1536]{0:T(1024)S(1)} %add_rsqrt_fusion.1) | copy-start | bytes 18436
  88.1 34.6 %copy-start.10 = (bf16[768,192]{1,0:T(8,128)(2,1)}, bf16[768,192]{1,0:T(8,128)(2,1)S(1)}, u32[]{:S(2)}) copy-start(bf16[768,192]{1,0:T(8,128)(2,1)S(1)} %all_gather.24) | copy-start | bytes 884740
  121.8 61.9 %copy-start.21 = (bf16[1536,192]{0,1:T(8,128)(2,1)}, bf16[1536,192]{0,1:T(8,128)(2,1)S(1)}, u32[]{:S(2)}) copy-start(bf16[1536,192]{0,1:T(8,128)(2,1)S(1)} %convolution_convert_fusion.2) | copy-start | bytes 1769476
  127.9 33.3 %collective-permute-start.1 = (bf16[96,192]{1,0:T(8,128)(2,1)}, bf16[96,192]{1,0:T(8,128)(2,1)}, u32[]{:S(2)}, u32[]{:S(2)}) collective-permute-start(bf16[96,192]{1,0:T(8,128)(2,1)} %collective-permute-done), channel_id=1, source_target_pairs={{0,4},{4,8},{8,12},{12,16},{16,20},{20,24},{24,28},{28,0},{1,5},{5... | collective-permute-start | bytes 110600 | tf_op jit(solution)/shard_map/ppermute | solution.py:23
  161.3 7.0 collective-permute-start.2
  163.2 8.1 %collective-permute-start.5 = (bf16[96,192]{1,0:T(8,128)(2,1)}, bf16[96,192]{1,0:T(8,128)(2,1)S(1)}, u32[]{:S(2)}, u32[]{:S(2)}) collective-permute-start(bf16[96,192]{1,0:T(8,128)(2,1)} %collective-permute-done.4), channel_id=1, source_target_pairs={{4,0},{8,4},{12,8},{16,12},{20,16},{24,20},{28,24},{0,28},{5,1},{9... | collective-permute-start | bytes 110600 | tf_op jit(solution)/shard_map/ppermute | solution.py:25
  168.3 7.9 %collective-permute-start.3 = (bf16[96,192]{1,0:T(8,128)(2,1)S(1)}, bf16[96,192]{1,0:T(8,128)(2,1)S(1)}, u32[]{:S(2)}, u32[]{:S(2)}) collective-permute-start(bf16[96,192]{1,0:T(8,128)(2,1)S(1)} %collective-permute-done.2), channel_id=1, source_target_pairs={{0,4},{4,8},{8,12},{12,16},{16,20},{20,24},{24,28},{28,0},{1,5},{5... | collective-permute-start | bytes 110600 | tf_op jit(solution)/shard_map/ppermute | solution.py:23
  171.3 12.5 %collective-permute-start.6 = (bf16[96,192]{1,0:T(8,128)(2,1)S(1)}, bf16[96,192]{1,0:T(8,128)(2,1)S(1)}, u32[]{:S(2)}, u32[]{:S(2)}) collective-permute-start(bf16[96,192]{1,0:T(8,128)(2,1)S(1)} %collective-permute-done.5), channel_id=1, source_target_pairs={{4,0},{8,4},{12,8},{16,12},{20,16},{24,20},{28,24},{0,28},{5,1},{9... | collective-permute-start | bytes 110600 | tf_op jit(solution)/shard_map/ppermute | solution.py:25
  186.0 6.2 copy-start.8
  188.8 13.8 %copy-start.37 = (bf16[512,192]{0,1:T(8,128)(2,1)}, bf16[512,192]{0,1:T(8,128)(2,1)S(1)}, u32[]{:S(2)}) copy-start(bf16[512,192]{0,1:T(8,128)(2,1)S(1)} %get-tuple-element.228) | copy-start | bytes 589828
  196.1 6.5 copy-start.7
  196.1 6.5 copy-start.54
  208.4 6.9 copy-start.57
  208.8 6.5 copy-start.14
  218.4 99.1 %all-gather.5.cloned.1.call-start = ((), (), s32[]{:S(2)}) async-start(), calls=%async_computation.9 | async-start | bytes 1327104 | tf_op jit(solution)/shard_map/all_gather | solution.py:188
  218.9 104.7 %all-gather.7.cloned.1.call-start = ((), (), s32[]{:S(2)}) async-start(), calls=%async_computation.10 | async-start | bytes 1327104 | tf_op jit(solution)/shard_map/all_gather | solution.py:189
  219.5 211.1 %all-reduce.9.cloned.1.call-start = ((), (), s32[]{:S(2)}) async-start(), calls=%async_computation.11 | async-start | bytes 9437184 | tf_op jit(solution)/shard_map/psum | solution.py:236
  323.6 8.5 %copy-start.68 = (bf16[768,768]{1,0:T(8,128)(2,1)S(1)}, bf16[768,768]{1,0:T(8,128)(2,1)}, u32[]{:S(2)}) copy-start(bf16[768,768]{1,0:T(8,128)(2,1)} %all-gather.5.cloned.1.call-done) | copy-start | bytes 3538948
  345.8 204.1 %all-to-all-start.5 = ((bf16[8,768,96]{1,2,0:T(8,128)(2,1)}), bf16[8,768,96]{1,2,0:T(8,128)(2,1)}, u32[]{:S(2)}, u32[]{:S(2)}) async-start(bf16[8,768,96]{1,2,0:T(8,128)(2,1)} %bitcast.177), calls=%async_computation.5 | async-start | bytes 2359296 | tf_op jit(solution)/shard_map/all_to_all | solution.py:40
  458.1 9.1 %copy-start.26 = (bf16[512,192]{0,1:T(8,128)(2,1)S(1)}, bf16[512,192]{0,1:T(8,128)(2,1)}, u32[]{:S(2)}) copy-start(bf16[512,192]{0,1:T(8,128)(2,1)} %get-tuple-element.224) | copy-start | bytes 589828
  472.3 26.9 %copy-start.24 = (pred[512,1024]{1,0:T(8,128)(4,1)S(1)}, pred[512,1024]{1,0:T(8,128)(4,1)}, u32[]{:S(2)}) copy-start(pred[512,1024]{1,0:T(8,128)(4,1)} %compare_and_fusion) | copy-start | bytes 1572868
  472.3 26.9 %copy-start.64 = (f32[3,512]{1,0:T(4,128)S(1)}, f32[3,512]{1,0:T(4,128)}, u32[]{:S(2)}) copy-start(f32[3,512]{1,0:T(4,128)} %log_add_fusion.1) | copy-start | bytes 18436
  532.2 8.0 %copy-start.17 = (pred[512,1536]{1,0:T(8,128)(4,1)S(1)}, pred[512,1536]{1,0:T(8,128)(4,1)}, u32[]{:S(2)}) copy-start(pred[512,1536]{1,0:T(8,128)(4,1)} %fusion.50) | copy-start | bytes 2359300
  532.2 8.0 %copy-start.27 = (bf16[512,192]{0,1:T(8,128)(2,1)S(1)}, bf16[512,192]{0,1:T(8,128)(2,1)}, u32[]{:S(2)}) copy-start(bf16[512,192]{0,1:T(8,128)(2,1)} %get-tuple-element.224) | copy-start | bytes 589828
  540.1 15.3 %copy-start.42 = (bf16[512,192]{0,1:T(8,128)(2,1)S(1)}, bf16[512,192]{0,1:T(8,128)(2,1)}, u32[]{:S(2)}) copy-start(bf16[512,192]{0,1:T(8,128)(2,1)} %slice.339) | copy-start | bytes 589828
  549.9 54.7 %all-to-all-start.4 = ((bf16[8,96,768]{2,1,0:T(8,128)(2,1)}), bf16[8,96,768]{2,1,0:T(8,128)(2,1)}, u32[]{:S(2)}, u32[]{:S(2)}) async-start(bf16[8,96,768]{2,1,0:T(8,128)(2,1)} %bitcast.176), calls=%async_computation.4 | async-start | bytes 2359296 | tf_op jit(solution)/shard_map/all_to_all | solution.py:40
  555.4 9.8 %copy-start.38 = (bf16[512,192]{0,1:T(8,128)(2,1)S(1)}, bf16[512,192]{0,1:T(8,128)(2,1)}, u32[]{:S(2)}) copy-start(bf16[512,192]{0,1:T(8,128)(2,1)} %copy-done.37) | copy-start | bytes 589828
  555.4 137.8 %all-reduce.11.cloned.1.call-start = ((), (), s32[]{:S(2)}) async-start(), calls=%async_computation.12 | async-start | bytes 9437184 | tf_op jit(solution)/shard_map/psum | solution.py:228
  565.1 27.8 %copy-start.13 = (bf16[768,192]{1,0:T(8,128)(2,1)S(1)}, bf16[768,192]{1,0:T(8,128)(2,1)}, u32[]{:S(2)}) copy-start(bf16[768,192]{1,0:T(8,128)(2,1)} %copy-done.12) | copy-start | bytes 884740
  604.5 16.9 %all-to-all-start.2 = ((bf16[8,96,192]{1,2,0:T(8,128)(2,1)}), bf16[8,96,192]{1,2,0:T(8,128)(2,1)S(1)}, u32[]{:S(2)}, u32[]{:S(2)}) async-start(bf16[8,96,192]{1,2,0:T(8,128)(2,1)} %copy.78), calls=%async_computation.2 | async-start | bytes 786432 | tf_op jit(solution)/shard_map/all_to_all | solution.py:40
  621.4 15.2 %all-to-all-start = ((bf16[8,96,192]{1,2,0:T(8,128)(2,1)}), bf16[8,96,192]{1,2,0:T(8,128)(2,1)}, u32[]{:S(2)}, u32[]{:S(2)}) async-start(bf16[8,96,192]{1,2,0:T(8,128)(2,1)} %copy.74), calls=%async_computation | async-start | bytes 786432 | tf_op jit(solution)/shard_map/all_to_all | solution.py:40
  636.6 14.9 %all-to-all-start.1 = ((bf16[8,96,192]{1,2,0:T(8,128)(2,1)}), bf16[8,96,192]{1,2,0:T(8,128)(2,1)}, u32[]{:S(2)}, u32[]{:S(2)}) async-start(bf16[8,96,192]{1,2,0:T(8,128)(2,1)} %copy.76), calls=%async_computation.1 | async-start | bytes 786432 | tf_op jit(solution)/shard_map/all_to_all | solution.py:40
  642.9 50.4 %copy-start.36 = (f32[1536]{0:T(1024)S(1)}, f32[1536]{0:T(1024)}, u32[]{:S(2)}) copy-start(f32[1536]{0:T(1024)} %copy-done.35) | copy-start | bytes 18436
  642.9 50.4 %copy-start.47 = (f32[1536]{0:T(1024)S(1)}, f32[1536]{0:T(1024)}, u32[]{:S(2)}) copy-start(f32[1536]{0:T(1024)} %copy-done.46) | copy-start | bytes 18436
  646.6 46.6 %copy-start.49 = (f32[768]{0:T(1024)S(1)}, f32[768]{0:T(1024)}, u32[]{:S(2)}) copy-start(f32[768]{0:T(1024)} %copy-done.48) | copy-start | bytes 9220
  651.5 14.8 %all-to-all-start.3 = ((bf16[8,192,96]{2,1,0:T(8,128)(2,1)}), bf16[8,192,96]{2,1,0:T(8,128)(2,1)S(1)}, u32[]{:S(2)}, u32[]{:S(2)}) async-start(bf16[8,192,96]{2,1,0:T(8,128)(2,1)} %bitcast.158), calls=%async_computation.3 | async-start | bytes 786432 | tf_op jit(solution)/shard_map/all_to_all | solution.py:40
  659.0 46.4 %copy-start.58 = (f32[1536]{0:T(1024)S(1)}, f32[1536]{0:T(1024)}, u32[]{:S(2)}) copy-start(f32[1536]{0:T(1024)} %fusion.153) | copy-start | bytes 18436
  693.2 17.4 %slice-start = ((s8[4718592]{0:T(1024)(128)(4,1)}), s8[524288]{0:T(1024)(128)(4,1)S(1)}, s32[]{:S(2)}) async-start(s8[4718592]{0:T(1024)(128)(4,1)} %bitcast.164), calls=%async_computation.13 | async-start | bytes 1048576
  699.8 14.6 %all-to-all-start.7 = ((bf16[8,2,96]{2,1,0:T(2,128)(2,1)}), bf16[8,2,96]{2,1,0:T(2,128)(2,1)S(1)}, u32[]{:S(2)}, u32[]{:S(2)}) async-start(bf16[8,2,96]{2,1,0:T(2,128)(2,1)} %copy.82), calls=%async_computation.7 | async-start | bytes 8192 | tf_op jit(solution)/shard_map/all_to_all | solution.py:40
  714.4 12.5 %all-to-all-start.6 = ((bf16[8,2,96]{2,1,0:T(2,128)(2,1)}), bf16[8,2,96]{2,1,0:T(2,128)(2,1)S(1)}, u32[]{:S(2)}, u32[]{:S(2)}) async-start(bf16[8,2,96]{2,1,0:T(2,128)(2,1)} %copy.81), calls=%async_computation.6 | async-start | bytes 8192 | tf_op jit(solution)/shard_map/all_to_all | solution.py:40
  (44 other events, 160.9 us)
Sparse Core Ops, SparseCore 0:
  218.5 91.3 all-reduce.6
  336.4 94.1 all-reduce.8
  598.4 94.7 all-reduce.10
Sparse Core Ops, SparseCore 1:
  221.0 38.7 all-gather.4
  261.9 40.0 all-gather.6
